TPU v7x, 32 devices: a whole 2x2x4 slice. The times are simulated.
32 devices in a mesh: sub: 8 (over y, x, core), coarse: 4 (over z).
Axes of the slice: x: 2, y: 2, z: 4, core: 2. Of those that a mesh axis runs over, the one named last changes fastest.
Arguments:
- right_side: float32 [8, 4, 128, 128], P('sub', 'coarse'), may hold values from -150 to 150
- diagonal: float32 [8, 4, 128, 128], P('sub', 'coarse'), may hold values from 2 to 8
- cell_link: float32 [8, 4, 128, 128], P('sub', 'coarse'), may hold values from 0.2 to 0.9
- block_inverse: float32 [8, 4, 128, 128, 128], P('sub', 'coarse'), may hold values from -1 to 1
- coupling: float32 [8, 4, 4, 128, 128], P('sub', 'coarse'), may hold values from -0.26516503 to 0.26516503
- coarse_basis: float32 [8, 4, 128, 128], P('sub', 'coarse'), may hold values from -6 to 6
- coarse_inverse: float32 [512, 512], P('coarse'), may hold values from -0.25 to 0.25
- partner: int32 [8, 4], P('sub'), may hold values from 0 to 7, as said below
- margin_width: int32 [8, 4], P('sub'), may hold values from 4 to 8, as said below
- margin_blocks: int32 [8, 4, 4, 8], P('sub', 'coarse'), may hold values from 0 to 127
- aggregate: int32 [8, 4, 128], P('sub', 'coarse'), may hold values from 0 to 511, as said below
Outputs:
- solution: float32 [8, 4, 128, 128], P('sub', 'coarse')
Inputs may be any that keep to these rules, and one draw needn't show every extreme that they name: partner[s, r] differs from s, partner[partner[s, r], r] = s, and the 4 partners of one subdomain are distinct. margin_width[partner[s, r], r] = margin_width[s, r]; every colour round has a pair with width 8. `margin_blocks`: entries with w >= margin_width[s, r] are not used. aggregate[s, c, b] lies in (s * 4 + c) * 16 to (s * 4 + c + 1) * 16 - 1, and every one of these 16 aggregates has a block of part [s, c].
All inputs are finite; a program needn't handle non-finite values.
Results may differ from a plain program's by a relative error of at most 0.0003.
Values sent between devices are 32-bit elements; how exact they have to be, the bound alone decides.
No kernel may reach another device: no remote copies, remote signals or barrier semaphores. Data moves between devices by JAX's collectives and lax.ppermute only.
A program may use at most 64 MiB of HBM per device.

v0:
```python
import jax
import jax.numpy as jnp
from jax import lax
from jax.sharding import PartitionSpec as P

BS = 128
BPD = 128
AGG_DEV = 16
ITERS = 4


def givens_solve(columns, beta):
    steps_count = len(columns)
    cosines = []
    sines = []
    side_terms = [beta] + [jnp.zeros_like(beta) for unused in range(steps_count)]
    triangle = []
    for column_id in range(steps_count):
        column = list(columns[column_id])
        for row_id in range(column_id):
            upper = column[row_id]
            lower = column[row_id + 1]
            column[row_id] = cosines[row_id] * upper + sines[row_id] * lower
            column[row_id + 1] = cosines[row_id] * lower - sines[row_id] * upper
        upper = column[column_id]
        lower = column[column_id + 1]
        radius = jnp.sqrt(upper * upper + lower * lower)
        cosine = upper / radius
        sine_value = lower / radius
        column[column_id] = radius
        cosines.append(cosine)
        sines.append(sine_value)
        side_terms[column_id + 1] = -sine_value * side_terms[column_id]
        side_terms[column_id] = cosine * side_terms[column_id]
        triangle.append(column)
    weights = [None] * steps_count
    for column_id in reversed(range(steps_count)):
        running = side_terms[column_id]
        for later_col in range(column_id + 1, steps_count):
            running = running - triangle[later_col][column_id] * weights[later_col]
        weights[column_id] = running / triangle[column_id][column_id]
    return weights


def on_device(
    right_side,
    diagonal,
    cell_link,
    block_inverse,
    coupling,
    coarse_basis,
    coarse_inverse,
    partner,
    margin_width,
    margin_blocks,
    aggregate,
):
    highest = lax.Precision.HIGHEST
    block_count = right_side.shape[2]
    unknowns = right_side.shape[3]
    factor = (BS * BPD / AGG_DEV) ** (-0.5)
    inverse_blocks = block_inverse[0, 0]
    couplings = coupling[0, 0]
    basis_local = coarse_basis[0, 0]
    diagonal_local = diagonal[0, 0]
    link_local = cell_link[0, 0]
    paired = partner[0]
    widths = margin_width[0]
    blocks = margin_blocks[0, 0]
    member_of = aggregate[0, 0]
    aggregate_count = coarse_inverse.shape[1]
    member_table = (member_of[:, None] == jnp.arange(aggregate_count)[None, :]).astype(jnp.float32)
    rounds = blocks.shape[0]
    widest = blocks.shape[1]
    target = (blocks.reshape(-1)[:, None] == jnp.arange(block_count)[None, :]).astype(jnp.float32)
    live_mask = (jnp.arange(widest)[None, :] < widths[:, None]).astype(jnp.float32)

    def margin(values):
        outgoing = jnp.take(values, blocks.reshape(-1), axis=0).reshape(rounds, widest, unknowns)
        pieces = []
        for round_id in range(rounds):
            gathered = lax.all_gather(outgoing[round_id], "sub", axis=0, tiled=True)
            pieces.append(lax.dynamic_slice_in_dim(gathered, paired[round_id] * widest, widest, 0))
        incoming = jnp.stack(pieces)
        mapped = (
            jnp.einsum("rij,rwj->rwi", couplings, incoming, precision=highest)
            * live_mask[:, :, None]
        )
        return jnp.einsum(
            "kb,ki->bi", target, mapped.reshape(rounds * widest, unknowns), precision=highest
        )

    def squared_norm(values):
        return lax.psum(jnp.sum(values * values), ("sub", "coarse"))

    start_vector = right_side[0, 0]
    directions = []
    columns = []
    beta = jnp.sqrt(squared_norm(start_vector))
    basis_list = [start_vector / beta]
    for krylov_step in range(ITERS):
        current = basis_list[-1]
        inner = jnp.sum(basis_local * current, axis=1)
        restricted = lax.psum(
            jnp.dot(inner, member_table, precision=highest) * factor, ("sub", "coarse")
        )
        local_part = jnp.einsum(
            "bij,bj->bi", inverse_blocks, current + margin(current), precision=highest
        )
        coarse_part = jnp.dot(coarse_inverse, restricted, precision=highest)
        coarse_full = lax.all_gather(coarse_part, "coarse", axis=0, tiled=True)
        prolonged = jnp.dot(member_table, coarse_full, precision=highest)
        direction = local_part + prolonged[:, None] * basis_local
        directions.append(direction)
        flat_line = direction.reshape(-1)
        link_line = link_local.reshape(-1)
        zero_pad = jnp.zeros((1,), jnp.float32)
        ahead_terms = jnp.concatenate([flat_line[1:], zero_pad]) * link_line
        behind_terms = jnp.concatenate([zero_pad, (link_line * flat_line)[:-1]])
        product = (
            diagonal_local * direction
            - (ahead_terms + behind_terms).reshape(direction.shape)
            - margin(direction)
        )
        projected = lax.psum(
            jnp.stack([jnp.sum(vector * product) for vector in basis_list]), ("sub", "coarse")
        )
        for position in range(len(basis_list)):
            product = product - projected[position] * basis_list[position]
        norm_new = jnp.sqrt(squared_norm(product))
        columns.append([projected[position] for position in range(len(basis_list))] + [norm_new])
        basis_list.append(product / norm_new)
    weights = givens_solve(columns, beta)
    solution = weights[0] * directions[0]
    for position in range(1, ITERS):
        solution = solution + weights[position] * directions[position]
    return solution.reshape(right_side.shape)


def solution(mesh):
    placed = (
        P("sub", "coarse", None, None),
        P("sub", "coarse", None, None),
        P("sub", "coarse", None, None),
        P("sub", "coarse", None, None, None),
        P("sub", "coarse", None, None, None),
        P("sub", "coarse", None, None),
        P("coarse", None),
        P("sub", None),
        P("sub", None),
        P("sub", "coarse", None, None),
        P("sub", "coarse", None),
    )
    return jax.shard_map(
        on_device,
        mesh=mesh,
        in_specs=placed,
        out_specs=P("sub", "coarse", None, None),
        check_vma=False,
    )
```

profile of v0, /device:TPU:0, one launch (start us, length us, event | category | flops | bytes accessed | tf_op | source)
XLA Modules:
  0.0 958.9 jit_solution(15861982066872133460)
XLA Ops:
  0.9 1.5 multiply_reduce_fusion.14
  2.3 42.2 %psum.91 = f32[]{:T(128)} all-reduce(f32[]{:T(128)} %multiply_reduce_fusion.14), channel_id=1, replica_groups=mesh['sub'=8,'coarse'=4] {'sub','coarse'}, use_global_device_ids=true, to_apply=%region_1.0 | all-reduce | flops 1 | bytes 8 | tf_op jit(solution)/shard_map/psum | solution.py:94
  46.9 10.0 %all_gather.108 = f32[64,128]{1,0:T(8,128)S(1)} all-gather(f32[8,128]{1,0:T(8,128)S(1)} %get-tuple-element.63), channel_id=1, replica_groups=mesh['sub'=8,'coarse'=4] {'sub'}, dimensions={0}, use_global_device_ids=true | all-gather | bytes 36864 | tf_op jit(solution)/shard_map/all_gather | solution.py:82
  56.9 1.5 fusion.188
  59.0 8.1 all_gather.109
  67.9 9.1 all_gather.110
  77.6 8.1 all_gather.111
  87.8 15.4 %fusion.6 = f32[128,1,128]{2,1,0:T(1,128)S(1)} fusion(f32[128,128,1]{1,2,0:T(1,128)S(1)} %bitcast.355, f32[1,1,128,128,128]{4,3,2,1,0:T(8,128)} %param.16), kind=kOutput, calls=%fused_computation.14 | convolution fusion | flops 25165824 | bytes 8519680 | tf_op jit(solution)/shard_map/bij,bj->bi/dot_general | solution.py:107
  103.5 39.4 %psum.92 = f32[512]{0:T(512)S(1)} all-reduce(f32[512]{0:T(512)S(1)} %broadcast_multiply_fusion.3), channel_id=1, replica_groups=mesh['sub'=8,'coarse'=4] {'sub','coarse'}, use_global_device_ids=true, to_apply=%region_3.5 | all-reduce | flops 512 | bytes 4096 | tf_op jit(solution)/shard_map/psum | solution.py:104
  143.1 9.8 %all-gather = f32[4,1,128]{2,1,0:T(1,128)S(1)} all-gather(f32[1,1,128]{2,1,0:T(1,128)S(1)} %convolution_bitcast_fusion.7), channel_id=1, replica_groups=mesh['sub'=8,'coarse'=4] {'coarse'}, dimensions={0}, use_global_device_ids=true | all-gather | bytes 2560 | tf_op jit(solution)/shard_map/all_gather | solution.py:111
  153.9 9.8 %all_gather.113 = f32[64,128]{1,0:T(8,128)S(1)} all-gather(f32[8,128]{1,0:T(8,128)S(1)} %get-tuple-element.59), channel_id=1, replica_groups=mesh['sub'=8,'coarse'=4] {'sub'}, dimensions={0}, use_global_device_ids=true | all-gather | bytes 36864 | tf_op jit(solution)/shard_map/all_gather | solution.py:82
  163.8 9.1 all_gather.114
  172.8 8.1 all_gather.115
  180.9 9.1 all_gather.116
  191.5 37.8 %psum.93 = f32[]{:T(128)} all-reduce(f32[]{:T(128)} %get-tuple-element.80), channel_id=1, replica_groups=mesh['sub'=8,'coarse'=4] {'sub','coarse'}, use_global_device_ids=true, to_apply=%region_5.7 | all-reduce | flops 1 | bytes 8 | tf_op jit(solution)/shard_map/psum | solution.py:125
  229.3 1.3 multiply_reduce_fusion.12
  230.6 41.2 %psum.94 = f32[]{:T(128)} all-reduce(f32[]{:T(128)} %multiply_reduce_fusion.12), channel_id=1, replica_groups=mesh['sub'=8,'coarse'=4] {'sub','coarse'}, use_global_device_ids=true, to_apply=%region_7.9 | all-reduce | flops 1 | bytes 8 | tf_op jit(solution)/shard_map/psum | solution.py:94
  274.0 10.1 %all_gather.117 = f32[64,128]{1,0:T(8,128)S(1)} all-gather(f32[8,128]{1,0:T(8,128)S(1)} %get-tuple-element.55), channel_id=1, replica_groups=mesh['sub'=8,'coarse'=4] {'sub'}, dimensions={0}, use_global_device_ids=true | all-gather | bytes 36864 | tf_op jit(solution)/shard_map/all_gather | solution.py:82
  284.1 9.0 all_gather.118
  293.1 8.1 all_gather.119
  301.2 9.0 all_gather.120
  311.1 15.4 %fusion.4 = f32[128,1,128]{2,1,0:T(1,128)S(1)} fusion(f32[128,128,1]{1,2,0:T(1,128)S(1)} %bitcast.356, f32[1,1,128,128,128]{4,3,2,1,0:T(8,128)} %param.16), kind=kOutput, calls=%fused_computation.12 | convolution fusion | flops 25165824 | bytes 8519680 | tf_op jit(solution)/shard_map/bij,bj->bi/dot_general | solution.py:107
  326.8 37.7 %psum.95 = f32[512]{0:T(512)S(1)} all-reduce(f32[512]{0:T(512)S(1)} %broadcast_multiply_fusion.2), channel_id=1, replica_groups=mesh['sub'=8,'coarse'=4] {'sub','coarse'}, use_global_device_ids=true, to_apply=%region_9.11 | all-reduce | flops 512 | bytes 4096 | tf_op jit(solution)/shard_map/psum | solution.py:104
  364.7 9.6 %all-gather.1 = f32[4,1,128]{2,1,0:T(1,128)S(1)} all-gather(f32[1,1,128]{2,1,0:T(1,128)S(1)} %convolution_bitcast_fusion.5), channel_id=1, replica_groups=mesh['sub'=8,'coarse'=4] {'coarse'}, dimensions={0}, use_global_device_ids=true | all-gather | bytes 2560 | tf_op jit(solution)/shard_map/all_gather | solution.py:111
  375.4 9.8 %all_gather.122 = f32[64,128]{1,0:T(8,128)S(1)} all-gather(f32[8,128]{1,0:T(8,128)S(1)} %get-tuple-element.51), channel_id=1, replica_groups=mesh['sub'=8,'coarse'=4] {'sub'}, dimensions={0}, use_global_device_ids=true | all-gather | bytes 36864 | tf_op jit(solution)/shard_map/all_gather | solution.py:82
  385.2 8.1 all_gather.123
  393.3 9.0 all_gather.124
  402.3 8.3 all_gather.125
  411.2 1.0 multiply_reduce_fusion.11
  412.2 1.3 pad_maximum_fusion.8
  413.5 37.6 %psum.96 = f32[2]{0:T(128)S(1)} all-reduce(f32[2]{0:T(128)S(1)} %pad_maximum_fusion.8), channel_id=1, replica_groups=mesh['sub'=8,'coarse'=4] {'sub','coarse'}, use_global_device_ids=true, to_apply=%region_12.14 | all-reduce | flops 2 | bytes 16 | tf_op jit(solution)/shard_map/psum | solution.py:125
  451.8 1.9 multiply_reduce_fusion.9
  453.6 41.7 %psum.97 = f32[]{:T(128)} all-reduce(f32[]{:T(128)} %get-tuple-element.21), channel_id=1, replica_groups=mesh['sub'=8,'coarse'=4] {'sub','coarse'}, use_global_device_ids=true, to_apply=%region_14.16 | all-reduce | flops 1 | bytes 8 | tf_op jit(solution)/shard_map/psum | solution.py:94
  496.8 10.1 %all_gather.126 = f32[64,128]{1,0:T(8,128)S(1)} all-gather(f32[8,128]{1,0:T(8,128)S(1)} %get-tuple-element.47), channel_id=1, replica_groups=mesh['sub'=8,'coarse'=4] {'sub'}, dimensions={0}, use_global_device_ids=true | all-gather | bytes 36864 | tf_op jit(solution)/shard_map/all_gather | solution.py:82
  506.9 8.1 all_gather.127
  515.0 9.0 all_gather.128
  524.0 8.1 all_gather.129
  533.0 15.4 %fusion.2 = f32[128,1,128]{2,1,0:T(1,128)S(1)} fusion(f32[128,128,1]{1,2,0:T(1,128)S(1)} %bitcast.357, f32[1,1,128,128,128]{4,3,2,1,0:T(8,128)} %param.16), kind=kOutput, calls=%fused_computation.10 | convolution fusion | flops 25165824 | bytes 8519680 | tf_op jit(solution)/shard_map/bij,bj->bi/dot_general | solution.py:107
  548.6 37.7 %psum.98 = f32[512]{0:T(512)S(1)} all-reduce(f32[512]{0:T(512)S(1)} %broadcast_multiply_fusion.1), channel_id=1, replica_groups=mesh['sub'=8,'coarse'=4] {'sub','coarse'}, use_global_device_ids=true, to_apply=%region_16.18 | all-reduce | flops 512 | bytes 4096 | tf_op jit(solution)/shard_map/psum | solution.py:104
  586.5 9.6 %all-gather.2 = f32[4,1,128]{2,1,0:T(1,128)S(1)} all-gather(f32[1,1,128]{2,1,0:T(1,128)S(1)} %convolution_bitcast_fusion.3), channel_id=1, replica_groups=mesh['sub'=8,'coarse'=4] {'coarse'}, dimensions={0}, use_global_device_ids=true | all-gather | bytes 2560 | tf_op jit(solution)/shard_map/all_gather | solution.py:111
  597.2 9.8 %all_gather.131 = f32[64,128]{1,0:T(8,128)S(1)} all-gather(f32[8,128]{1,0:T(8,128)S(1)} %get-tuple-element.43), channel_id=1, replica_groups=mesh['sub'=8,'coarse'=4] {'sub'}, dimensions={0}, use_global_device_ids=true | all-gather | bytes 36864 | tf_op jit(solution)/shard_map/all_gather | solution.py:82
  607.0 9.0 all_gather.132
  616.1 8.5 all_gather.133
  624.6 9.0 all_gather.134
  635.2 1.9 pad_maximum_fusion.9
  637.2 37.6 %psum.99 = f32[3]{0:T(128)S(1)} all-reduce(f32[3]{0:T(128)S(1)} %pad_maximum_fusion.9), channel_id=1, replica_groups=mesh['sub'=8,'coarse'=4] {'sub','coarse'}, use_global_device_ids=true, to_apply=%region_20.22 | all-reduce | flops 3 | bytes 24 | tf_op jit(solution)/shard_map/psum | solution.py:125
  675.4 2.5 multiply_reduce_fusion.5
  677.9 40.7 %psum.100 = f32[]{:T(128)} all-reduce(f32[]{:T(128)} %get-tuple-element.17), channel_id=1, replica_groups=mesh['sub'=8,'coarse'=4] {'sub','coarse'}, use_global_device_ids=true, to_apply=%region_22.24 | all-reduce | flops 1 | bytes 8 | tf_op jit(solution)/shard_map/psum | solution.py:94
  720.0 10.0 %all_gather.135 = f32[64,128]{1,0:T(8,128)S(1)} all-gather(f32[8,128]{1,0:T(8,128)S(1)} %get-tuple-element.39), channel_id=1, replica_groups=mesh['sub'=8,'coarse'=4] {'sub'}, dimensions={0}, use_global_device_ids=true | all-gather | bytes 36864 | tf_op jit(solution)/shard_map/all_gather | solution.py:82
  730.0 9.0 all_gather.136
  739.1 8.1 all_gather.137
  747.1 9.0 all_gather.138
  757.1 15.4 %fusion = f32[128,1,128]{2,1,0:T(1,128)S(1)} fusion(f32[128,128,1]{1,2,0:T(1,128)S(1)} %bitcast.358, f32[1,1,128,128,128]{4,3,2,1,0:T(8,128)} %param.16), kind=kOutput, calls=%fused_computation.8 | convolution fusion | flops 25165824 | bytes 8519680 | tf_op jit(solution)/shard_map/bij,bj->bi/dot_general | solution.py:107
  772.7 37.7 %psum.101 = f32[512]{0:T(512)S(1)} all-reduce(f32[512]{0:T(512)S(1)} %broadcast_multiply_fusion), channel_id=1, replica_groups=mesh['sub'=8,'coarse'=4] {'sub','coarse'}, use_global_device_ids=true, to_apply=%region_24.26 | all-reduce | flops 512 | bytes 4096 | tf_op jit(solution)/shard_map/psum | solution.py:104
  810.6 9.6 %all-gather.3 = f32[4,1,128]{2,1,0:T(1,128)S(1)} all-gather(f32[1,1,128]{2,1,0:T(1,128)S(1)} %convolution_bitcast_fusion.1), channel_id=1, replica_groups=mesh['sub'=8,'coarse'=4] {'coarse'}, dimensions={0}, use_global_device_ids=true | all-gather | bytes 2560 | tf_op jit(solution)/shard_map/all_gather | solution.py:111
  821.3 9.8 %all_gather.140 = f32[64,128]{1,0:T(8,128)S(1)} all-gather(f32[8,128]{1,0:T(8,128)S(1)} %get-tuple-element.35), channel_id=1, replica_groups=mesh['sub'=8,'coarse'=4] {'sub'}, dimensions={0}, use_global_device_ids=true | all-gather | bytes 36864 | tf_op jit(solution)/shard_map/all_gather | solution.py:82
  831.1 8.2 all_gather.141
  839.4 9.0 all_gather.142
  848.4 8.1 all_gather.143
  857.1 1.0 multiply_reduce_fusion.4
  858.1 2.5 pad_maximum_fusion.10
  860.6 37.6 %psum.102 = f32[4]{0:T(128)S(1)} all-reduce(f32[4]{0:T(128)S(1)} %pad_maximum_fusion.10), channel_id=1, replica_groups=mesh['sub'=8,'coarse'=4] {'sub','coarse'}, use_global_device_ids=true, to_apply=%region_29.31 | all-reduce | flops 4 | bytes 32 | tf_op jit(solution)/shard_map/psum | solution.py:125
  905.5 3.0 multiply_reduce_fusion
  908.5 41.8 %psum.103 = f32[]{:T(128)} all-reduce(f32[]{:T(128)} %multiply_reduce_fusion), channel_id=1, replica_groups=mesh['sub'=8,'coarse'=4] {'sub','coarse'}, use_global_device_ids=true, to_apply=%region_31.33 | all-reduce | flops 1 | bytes 8 | tf_op jit(solution)/shard_map/psum | solution.py:94
  (119 shorter events, 22.8 us)
Async XLA Ops:
  0.0 87.0 %copy-start = (f32[1,1,4,128,128]{4,3,2,1,0:T(8,128)S(1)}, f32[1,1,4,128,128]{4,3,2,1,0:T(8,128)}, u32[]{:S(2)}) copy-start(f32[1,1,4,128,128]{4,3,2,1,0:T(8,128)} %param.17) | copy-start | bytes 786436
  0.0 153.1 %copy-start.1 = (f32[1,1,128,128]{3,2,1,0:T(8,128)S(1)}, f32[1,1,128,128]{3,2,1,0:T(8,128)}, u32[]{:S(2)}) copy-start(f32[1,1,128,128]{3,2,1,0:T(8,128)} %param.18) | copy-start | bytes 196612
  0.0 103.2 %copy-start.5 = (s32[1,1,128]{2,1,0:T(1,128)S(1)}, s32[1,1,128]{2,1,0:T(1,128)}, u32[]{:S(2)}) copy-start(s32[1,1,128]{2,1,0:T(1,128)} %param.23) | copy-start | bytes 1540
  0.0 142.9 %copy-start.2 = (f32[128,512]{1,0:T(8,128)S(1)}, f32[128,512]{1,0:T(8,128)}, u32[]{:S(2)}) copy-start(f32[128,512]{1,0:T(8,128)} %param.19) | copy-start | bytes 786436
  0.0 190.4 %copy-start.3 = (f32[1,1,128,128]{3,2,1,0:T(8,128)S(1)}, f32[1,1,128,128]{3,2,1,0:T(8,128)}, u32[]{:S(2)}) copy-start(f32[1,1,128,128]{3,2,1,0:T(8,128)} %param.15) | copy-start | bytes 196612
  0.0 190.5 %copy-start.4 = (f32[1,1,128,128]{3,2,1,0:T(8,128)S(1)}, f32[1,1,128,128]{3,2,1,0:T(8,128)}, u32[]{:S(2)}) copy-start(f32[1,1,128,128]{3,2,1,0:T(8,128)} %param.14) | copy-start | bytes 196612
where the time goes:
time: 971 us; the launch traced here: 959 us
  blocking collectives  835 us (86%)
  matrix products  73.9 us (8%)
  other arithmetic  21.1 us (2%)
  between operations  20.1 us (2%)
    all_gather x32, blocking collectives, margin(): gathered = lax.all_gather(outgoing[round_id], 'sub', axis=0, tiled=True)  286 us
    psum x5, blocking collectives, squared_norm(): return lax.psum(jnp.sum(values * values), ('sub', 'coarse'))  208 us
    psum x4, blocking collectives, on_device(): lax.psum(jnp.dot(inner, member_table, precision=highest) * factor, ('sub'...  152 us
    psum x4, blocking collectives, on_device(): lax.psum(jnp.stack([jnp.sum(vector * product) for vector in basis_list]),...  151 us
    dot_general x4, matrix products, on_device(): jnp.einsum('bij,bj->bi', inverse_blocks, current + margin(current), preci...  61.5 us
    all_gather x4, blocking collectives, on_device(): coarse_full = lax.all_gather(coarse_part, 'coarse', axis=0, tiled=True)  38.7 us

commit v1 on v0

--- a/solution.py
+++ b/solution.py
@@ -101,8 +101,11 @@
     for krylov_step in range(ITERS):
         current = basis_list[-1]
         inner = jnp.sum(basis_local * current, axis=1)
-        restricted = lax.psum(
-            jnp.dot(inner, member_table, precision=highest) * factor, ("sub", "coarse")
+        restricted = jnp.sum(
+            lax.all_gather(
+                jnp.dot(inner, member_table, precision=highest) * factor, ("sub", "coarse")
+            ),
+            axis=0,
         )
         local_part = jnp.einsum(
             "bij,bj->bi", inverse_blocks, current + margin(current), precision=highest

time: 971 us -> 1070 us (1.10)
  blocking collectives: 835 us -> 936 us
    all_gather x0 -> x4, blocking collectives: none -> 267 us  [on_device(): lax.all_gather(jnp.dot(inner, member_table, precision=highest) * factor,...]
    psum x4 -> x0, blocking collectives: 152 us -> none  [on_device(): lax.psum(jnp.dot(inner, member_table, precision=highest) * factor, ('sub'...]
where the time goes in v1:
time: 1070 us; the launch traced here: 1060 us
  blocking collectives  936 us (87%)
  matrix products  73.9 us (7%)
  other arithmetic  21.3 us (2%)
  between operations  20.1 us (2%)
    all_gather x32, blocking collectives, margin(): gathered = lax.all_gather(outgoing[round_id], 'sub', axis=0, tiled=True)  278 us
    all_gather x4, blocking collectives, on_device(): lax.all_gather(jnp.dot(inner, member_table, precision=highest) * factor,...  267 us
    psum x5, blocking collectives, squared_norm(): return lax.psum(jnp.sum(values * values), ('sub', 'coarse'))  201 us
    psum x4, blocking collectives, on_device(): lax.psum(jnp.stack([jnp.sum(vector * product) for vector in basis_list]),...  160 us
    dot_general x4, matrix products, on_device(): jnp.einsum('bij,bj->bi', inverse_blocks, current + margin(current), preci...  61.5 us
    all_gather x4, blocking collectives, on_device(): coarse_full = lax.all_gather(coarse_part, 'coarse', axis=0, tiled=True)  30.2 us

profile of v1, /device:TPU:0, one launch (start us, length us, event | category | flops | bytes accessed | tf_op | source)
XLA Modules:
  0.0 1060.0 jit_solution(2502491910254648364)
XLA Ops:
  0.9 1.5 multiply_reduce_fusion.14
  2.3 42.2 %psum.63 = f32[]{:T(128)} all-reduce(f32[]{:T(128)} %multiply_reduce_fusion.14), channel_id=1, replica_groups=mesh['sub'=8,'coarse'=4] {'sub','coarse'}, use_global_device_ids=true, to_apply=%region_1.0 | all-reduce | flops 1 | bytes 8 | tf_op jit(solution)/shard_map/psum | solution.py:94
  46.9 10.0 all_gather.132
  56.9 1.5 fusion.188
  59.0 8.1 all_gather.133
  67.9 9.1 all_gather.134
  77.6 8.1 all_gather.135
  87.8 15.4 %fusion.6 = f32[128,1,128]{2,1,0:T(1,128)S(1)} fusion(f32[128,128,1]{1,2,0:T(1,128)S(1)} %bitcast.359, f32[1,1,128,128,128]{4,3,2,1,0:T(8,128)} %param.16), kind=kOutput, calls=%fused_computation.14 | convolution fusion | flops 25165824 | bytes 8519680 | tf_op jit(solution)/shard_map/bij,bj->bi/dot_general | solution.py:110
  103.5 66.8 %all-gather.4 = f32[32,1,512]{2,1,0:T(1,128)S(1)} all-gather(f32[1,1,512]{2,1,0:T(1,128)S(1)} %bitcast.367), channel_id=2, replica_groups=mesh['sub'=8,'coarse'=4] {'sub','coarse'}, dimensions={0}, use_global_device_ids=true | all-gather | bytes 67584 | tf_op jit(solution)/shard_map/all_gather | solution.py:105
  170.7 7.6 all-gather.5
  179.3 9.0 all_gather.139
  188.3 8.1 all_gather.140
  196.4 9.0 all_gather.141
  205.4 8.1 all_gather.142
  215.1 40.1 %psum.64 = f32[]{:T(128)} all-reduce(f32[]{:T(128)} %get-tuple-element.80), channel_id=1, replica_groups=mesh['sub'=8,'coarse'=4] {'sub','coarse'}, use_global_device_ids=true, to_apply=%region_5.7 | all-reduce | flops 1 | bytes 8 | tf_op jit(solution)/shard_map/psum | solution.py:128
  255.2 1.3 multiply_reduce_fusion.12
  256.5 39.8 %psum.65 = f32[]{:T(128)} all-reduce(f32[]{:T(128)} %multiply_reduce_fusion.12), channel_id=1, replica_groups=mesh['sub'=8,'coarse'=4] {'sub','coarse'}, use_global_device_ids=true, to_apply=%region_7.9 | all-reduce | flops 1 | bytes 8 | tf_op jit(solution)/shard_map/psum | solution.py:94
  298.5 10.1 all_gather.143
  308.6 8.1 all_gather.144
  316.7 9.0 all_gather.145
  325.7 8.1 all_gather.146
  334.7 15.4 %fusion.4 = f32[128,1,128]{2,1,0:T(1,128)S(1)} fusion(f32[128,128,1]{1,2,0:T(1,128)S(1)} %bitcast.360, f32[1,1,128,128,128]{4,3,2,1,0:T(8,128)} %param.16), kind=kOutput, calls=%fused_computation.12 | convolution fusion | flops 25165824 | bytes 8519680 | tf_op jit(solution)/shard_map/bij,bj->bi/dot_general | solution.py:110
  350.4 66.7 %all-gather.6 = f32[32,1,512]{2,1,0:T(1,128)S(1)} all-gather(f32[1,1,512]{2,1,0:T(1,128)S(1)} %bitcast.368), channel_id=3, replica_groups=mesh['sub'=8,'coarse'=4] {'sub','coarse'}, dimensions={0}, use_global_device_ids=true | all-gather | bytes 67584 | tf_op jit(solution)/shard_map/all_gather | solution.py:105
  417.4 7.6 all-gather.7
  426.0 8.9 all_gather.150
  435.0 8.2 all_gather.151
  443.2 8.9 all_gather.152
  452.1 8.2 all_gather.153
  460.9 1.0 multiply_reduce_fusion.11
  461.9 1.3 pad_maximum_fusion.8
  463.2 40.1 %psum.66 = f32[2]{0:T(128)S(1)} all-reduce(f32[2]{0:T(128)S(1)} %pad_maximum_fusion.8), channel_id=1, replica_groups=mesh['sub'=8,'coarse'=4] {'sub','coarse'}, use_global_device_ids=true, to_apply=%region_12.14 | all-reduce | flops 2 | bytes 16 | tf_op jit(solution)/shard_map/psum | solution.py:128
  503.9 1.9 multiply_reduce_fusion.9
  505.8 39.5 %psum.67 = f32[]{:T(128)} all-reduce(f32[]{:T(128)} %get-tuple-element.21), channel_id=1, replica_groups=mesh['sub'=8,'coarse'=4] {'sub','coarse'}, use_global_device_ids=true, to_apply=%region_14.16 | all-reduce | flops 1 | bytes 8 | tf_op jit(solution)/shard_map/psum | solution.py:94
  546.8 10.1 all_gather.154
  556.9 8.2 all_gather.155
  565.1 8.9 all_gather.156
  574.0 8.2 all_gather.157
  583.0 15.4 %fusion.2 = f32[128,1,128]{2,1,0:T(1,128)S(1)} fusion(f32[128,128,1]{1,2,0:T(1,128)S(1)} %bitcast.361, f32[1,1,128,128,128]{4,3,2,1,0:T(8,128)} %param.16), kind=kOutput, calls=%fused_computation.10 | convolution fusion | flops 25165824 | bytes 8519680 | tf_op jit(solution)/shard_map/bij,bj->bi/dot_general | solution.py:110
  598.7 66.7 %all-gather.8 = f32[32,1,512]{2,1,0:T(1,128)S(1)} all-gather(f32[1,1,512]{2,1,0:T(1,128)S(1)} %bitcast.369), channel_id=4, replica_groups=mesh['sub'=8,'coarse'=4] {'sub','coarse'}, dimensions={0}, use_global_device_ids=true | all-gather | bytes 67584 | tf_op jit(solution)/shard_map/all_gather | solution.py:105
  665.7 7.6 all-gather.9
  674.3 9.0 all_gather.161
  683.3 8.1 all_gather.162
  691.4 9.0 all_gather.163
  700.4 8.1 all_gather.164
  710.1 1.9 pad_maximum_fusion.9
  712.1 39.9 %psum.68 = f32[3]{0:T(128)S(1)} all-reduce(f32[3]{0:T(128)S(1)} %pad_maximum_fusion.9), channel_id=1, replica_groups=mesh['sub'=8,'coarse'=4] {'sub','coarse'}, use_global_device_ids=true, to_apply=%region_20.22 | all-reduce | flops 3 | bytes 24 | tf_op jit(solution)/shard_map/psum | solution.py:128
  752.6 2.5 multiply_reduce_fusion.5
  755.1 39.5 %psum.69 = f32[]{:T(128)} all-reduce(f32[]{:T(128)} %get-tuple-element.17), channel_id=1, replica_groups=mesh['sub'=8,'coarse'=4] {'sub','coarse'}, use_global_device_ids=true, to_apply=%region_22.24 | all-reduce | flops 1 | bytes 8 | tf_op jit(solution)/shard_map/psum | solution.py:94
  796.0 10.0 all_gather.165
  806.0 8.1 all_gather.166
  814.2 9.0 all_gather.167
  823.2 8.1 all_gather.168
  832.1 15.4 %fusion = f32[128,1,128]{2,1,0:T(1,128)S(1)} fusion(f32[128,128,1]{1,2,0:T(1,128)S(1)} %bitcast.362, f32[1,1,128,128,128]{4,3,2,1,0:T(8,128)} %param.16), kind=kOutput, calls=%fused_computation.8 | convolution fusion | flops 25165824 | bytes 8519680 | tf_op jit(solution)/shard_map/bij,bj->bi/dot_general | solution.py:110
  847.8 66.7 %all-gather.10 = f32[32,1,512]{2,1,0:T(1,128)S(1)} all-gather(f32[1,1,512]{2,1,0:T(1,128)S(1)} %bitcast.370), channel_id=5, replica_groups=mesh['sub'=8,'coarse'=4] {'sub','coarse'}, dimensions={0}, use_global_device_ids=true | all-gather | bytes 67584 | tf_op jit(solution)/shard_map/all_gather | solution.py:105
  914.9 7.6 all-gather.11
  923.5 8.9 all_gather.172
  932.4 8.2 all_gather.173
  940.6 8.9 all_gather.174
  949.5 8.2 all_gather.175
  958.4 1.0 multiply_reduce_fusion.4
  959.4 2.5 pad_maximum_fusion.10
  961.9 39.7 %psum.70 = f32[4]{0:T(128)S(1)} all-reduce(f32[4]{0:T(128)S(1)} %pad_maximum_fusion.10), channel_id=1, replica_groups=mesh['sub'=8,'coarse'=4] {'sub','coarse'}, use_global_device_ids=true, to_apply=%region_29.31 | all-reduce | flops 4 | bytes 32 | tf_op jit(solution)/shard_map/psum | solution.py:128
  1008.8 3.0 multiply_reduce_fusion
  1011.8 39.5 %psum.71 = f32[]{:T(128)} all-reduce(f32[]{:T(128)} %multiply_reduce_fusion), channel_id=1, replica_groups=mesh['sub'=8,'coarse'=4] {'sub','coarse'}, use_global_device_ids=true, to_apply=%region_31.33 | all-reduce | flops 1 | bytes 8 | tf_op jit(solution)/shard_map/psum | solution.py:94
  (123 shorter events, 23.0 us)
Async XLA Ops:
  0.0 87.0 %copy-start = (f32[1,1,4,128,128]{4,3,2,1,0:T(8,128)S(1)}, f32[1,1,4,128,128]{4,3,2,1,0:T(8,128)}, u32[]{:S(2)}) copy-start(f32[1,1,4,128,128]{4,3,2,1,0:T(8,128)} %param.17) | copy-start | bytes 786436
  0.0 178.4 %copy-start.1 = (f32[1,1,128,128]{3,2,1,0:T(8,128)S(1)}, f32[1,1,128,128]{3,2,1,0:T(8,128)}, u32[]{:S(2)}) copy-start(f32[1,1,128,128]{3,2,1,0:T(8,128)} %param.18) | copy-start | bytes 196612
  0.0 103.2 %copy-start.5 = (s32[1,1,128]{2,1,0:T(1,128)S(1)}, s32[1,1,128]{2,1,0:T(1,128)}, u32[]{:S(2)}) copy-start(s32[1,1,128]{2,1,0:T(1,128)} %param.23) | copy-start | bytes 1540
  0.0 170.4 %copy-start.2 = (f32[128,512]{1,0:T(8,128)S(1)}, f32[128,512]{1,0:T(8,128)}, u32[]{:S(2)}) copy-start(f32[128,512]{1,0:T(8,128)} %param.19) | copy-start | bytes 786436
  0.0 214.0 %copy-start.3 = (f32[1,1,128,128]{3,2,1,0:T(8,128)S(1)}, f32[1,1,128,128]{3,2,1,0:T(8,128)}, u32[]{:S(2)}) copy-start(f32[1,1,128,128]{3,2,1,0:T(8,128)} %param.15) | copy-start | bytes 196612
  0.0 214.1 %copy-start.4 = (f32[1,1,128,128]{3,2,1,0:T(8,128)S(1)}, f32[1,1,128,128]{3,2,1,0:T(8,128)}, u32[]{:S(2)}) copy-start(f32[1,1,128,128]{3,2,1,0:T(8,128)} %param.14) | copy-start | bytes 196612
